TPU v7x, 32 devices: a whole 2x2x4 slice. The times are simulated.
32 devices in a mesh: dp: 8 (over z, y), rep: 4 (over x, core).
Axes of the slice: x: 2, y: 2, z: 4, core: 2. Of those that a mesh axis runs over, the one named last changes fastest.
Arguments:
- cell_input: bfloat16 [16384, 1024], P(('dp', 'rep')), may hold values from -6 to 6
- cotangent: bfloat16 [16384, 1024], P(('dp', 'rep')), may hold values from -6 to 6
- segment_ids: int32 [32, 512], P(('dp', 'rep')), may hold values from 0 to 15, never falling along the last dimension, each value on 1 to 128 neighbouring positions
- lengths: int32 [32], P(('dp', 'rep')), may hold values from 256 to 512
- w_qkv: bfloat16 [1024, 3072], P('dp'), may hold values from -0.1875 to 0.1875
- query_bias: bfloat16 [1024], P('dp'), may hold values from -1.75 to 1.75
- value_bias: bfloat16 [1024], P('dp'), may hold values from -1.75 to 1.75
- w_out: bfloat16 [1024, 1024], P('dp'), may hold values from -1 to 1
- out_bias: bfloat16 [1024], P('dp'), may hold values from -1.75 to 1.75
- w_up: bfloat16 [1024, 4096], P('dp'), may hold values from -0.1875 to 0.1875
- up_bias: bfloat16 [4096], P('dp'), may hold values from -1.75 to 1.75
- w_down: bfloat16 [4096, 1024], P('dp'), may hold values from -0.09375 to 0.09375
- down_bias: bfloat16 [1024], P('dp'), may hold values from -1.75 to 1.75
- norm1_gain: bfloat16 [1024], P('dp'), may hold values from 0.5 to 1.5
- norm1_bias: bfloat16 [1024], P('dp'), may hold values from -1.75 to 1.75
- norm2_gain: bfloat16 [1024], P('dp'), may hold values from 0.5 to 1.5
- norm2_bias: bfloat16 [1024], P('dp'), may hold values from -1.75 to 1.75
Outputs:
- block_out: bfloat16 [16384, 1024], P(('dp', 'rep'))
- input_grad: bfloat16 [16384, 1024], P(('dp', 'rep'))
- grad_qkv: float32 [1024, 3072], P('dp')
- grad_query_bias: float32 [1024], P('dp')
- grad_value_bias: float32 [1024], P('dp')
- grad_out: float32 [1024, 1024], P('dp')
- grad_out_bias: float32 [1024], P('dp')
- grad_up: float32 [1024, 4096], P('dp')
- grad_up_bias: float32 [4096], P('dp')
- grad_down: float32 [4096, 1024], P('dp')
- grad_down_bias: float32 [1024], P('dp')
- grad_norm1_gain: float32 [1024], P('dp')
- grad_norm1_bias: float32 [1024], P('dp')
- grad_norm2_gain: float32 [1024], P('dp')
- grad_norm2_bias: float32 [1024], P('dp')
Inputs may be any that keep to these rules, and one draw needn't show every extreme that they name: `segment_ids`: in each sequence the ids never fall; each of the 16 slides holds 1 to 128 cells, and one holds exactly 128. `lengths`: rows of a sequence at or past its length are padding.
All inputs are finite; a program needn't handle non-finite values.
Results may differ from a plain program's by a relative error of at most 0.015.
Values may be sent and summed in bfloat16 or wider, within the bound.
No kernel may reach another device: no remote copies, remote signals or barrier semaphores. Data moves between devices by JAX's collectives and lax.ppermute only.
A program may use at most 192 MiB of HBM per device.

v0:
```python
import math
import jax
import jax.numpy as jnp
from jax import lax
from jax.sharding import PartitionSpec as P

HEAD_DIM = 64


def normalize(values_in):
    row_mean = jnp.mean(values_in, axis=-1, keepdims=True)
    centred = values_in - row_mean
    inv_std = lax.rsqrt(jnp.mean(centred * centred, axis=-1, keepdims=True) + 1e-05)
    return (centred * inv_std, inv_std)


def norm_back(incoming, normed, inv_std, gain_vec):
    scaled = incoming * gain_vec
    return inv_std * (
        scaled
        - jnp.mean(scaled, axis=-1, keepdims=True)
        - normed * jnp.mean(scaled * normed, axis=-1, keepdims=True)
    )


def positions(length, model_width):
    places = jnp.arange(length, dtype=jnp.float32)[:, None]
    frequency = jnp.exp(
        jnp.arange(model_width // 2, dtype=jnp.float32) * (-2.0 * math.log(10000.0) / model_width)
    )
    angles = places * frequency[None, :]
    return jnp.stack([jnp.sin(angles), jnp.cos(angles)], axis=-1).reshape(length, model_width)


def gelu_slope(values_in):
    normal_cdf = 0.5 * (1.0 + lax.erf(values_in * (1.0 / math.sqrt(2.0))))
    return normal_cdf + values_in * jnp.exp(-0.5 * values_in * values_in) * (
        1.0 / math.sqrt(2.0 * math.pi)
    )


def block_mask(begin_row, block_rows, seg_row, live_cells):
    places = jnp.arange(seg_row.shape[0], dtype=jnp.int32)
    rows_at = begin_row + jnp.arange(block_rows, dtype=jnp.int32)
    return (seg_row[:, None] == seg_row[None, :]) & live_cells[:, None] & live_cells[None, :] | (
        rows_at[:, None] == places[None, :]
    )


def masked_scores(block_q, key_vecs, begin_row, block_rows, seg_row, live_cells):
    score_scale = 1.0 / math.sqrt(HEAD_DIM)
    scores = (
        jnp.einsum("qhd,khd->hqk", block_q, key_vecs, preferred_element_type=jnp.float32)
        * score_scale
    )
    return jnp.where(block_mask(begin_row, block_rows, seg_row, live_cells)[None], scores, -1e30)


def attention_forward(queries, key_vecs, values, seg_row, live_cells, block_rows):
    begin_rows = jnp.arange(queries.shape[0] // block_rows, dtype=jnp.int32) * block_rows

    def query_block(begin_row):
        scores = masked_scores(queries, key_vecs, begin_row, block_rows, seg_row, live_cells)
        row_max = jnp.max(scores, axis=-1, keepdims=True)
        exp_scores = jnp.exp(scores - row_max)
        row_total = jnp.sum(exp_scores, axis=-1, keepdims=True)
        weights = (exp_scores / row_total).astype(jnp.bfloat16)
        attended = jnp.einsum("hqk,khd->qhd", weights, values, preferred_element_type=jnp.float32)
        return (attended.astype(jnp.bfloat16), (row_max + jnp.log(row_total))[..., 0])

    attended, log_totals = lax.map(query_block, begin_rows)
    return (attended.reshape(queries.shape), log_totals)


def attention_backward(
    queries, key_vecs, values, attended_grad, log_totals, seg_row, live_cells, block_rows
):
    score_scale = 1.0 / math.sqrt(HEAD_DIM)
    begin_rows = jnp.arange(queries.shape[0] // block_rows, dtype=jnp.int32) * block_rows

    def query_block(running, inputs):
        begin_row, block_log = inputs
        key_total, value_total = running
        scores = masked_scores(queries, key_vecs, begin_row, block_rows, seg_row, live_cells)
        weights_f = jnp.exp(scores - block_log[..., None])
        value_total = value_total + jnp.einsum(
            "hqk,qhd->khd",
            weights_f.astype(jnp.bfloat16),
            attended_grad,
            preferred_element_type=jnp.float32,
        )
        prob_grad = jnp.einsum(
            "qhd,khd->hqk", attended_grad, values, preferred_element_type=jnp.float32
        )
        dscore = (
            weights_f * (prob_grad - jnp.sum(prob_grad * weights_f, axis=-1, keepdims=True))
        ).astype(jnp.bfloat16)
        block_dq = (
            jnp.einsum("hqk,khd->qhd", dscore, key_vecs, preferred_element_type=jnp.float32)
            * score_scale
        ).astype(jnp.bfloat16)
        key_total = (
            key_total
            + jnp.einsum("hqk,qhd->khd", dscore, queries, preferred_element_type=jnp.float32)
            * score_scale
        )
        return ((key_total, value_total), block_dq)

    zero_acc = jnp.zeros(queries.shape, jnp.float32)
    (key_total, value_total), query_grad = lax.scan(
        query_block, (zero_acc, zero_acc), (begin_rows, log_totals)
    )
    return (
        query_grad.reshape(queries.shape),
        key_total.astype(jnp.bfloat16),
        value_total.astype(jnp.bfloat16),
    )


def forward_pass(gathered, cell_input, pos_table, seg_row, live_cells, block_rows):
    (
        w_qkv,
        query_bias,
        value_bias,
        w_out,
        out_bias,
        w_up,
        up_bias,
        w_down,
        down_bias,
        norm1_gain,
        norm1_bias,
        norm2_gain,
        norm2_bias,
    ) = gathered
    length, model_width = cell_input.shape
    head_count = model_width // HEAD_DIM
    cells_f = cell_input.astype(jnp.float32)
    normed_one, inv_one = normalize(cells_f)
    normed_in = (
        normed_one * norm1_gain.astype(jnp.float32) + norm1_bias.astype(jnp.float32) + pos_table
    ).astype(jnp.bfloat16)
    projected = jnp.dot(normed_in, w_qkv, preferred_element_type=jnp.float32)
    queries = (
        (projected[:, :model_width] + query_bias.astype(jnp.float32))
        .astype(jnp.bfloat16)
        .reshape(length, head_count, HEAD_DIM)
    )
    key_vecs = (
        projected[:, model_width : 2 * model_width]
        .astype(jnp.bfloat16)
        .reshape(length, head_count, HEAD_DIM)
    )
    values = (
        (projected[:, 2 * model_width :] + value_bias.astype(jnp.float32))
        .astype(jnp.bfloat16)
        .reshape(length, head_count, HEAD_DIM)
    )
    attended, log_totals = attention_forward(
        queries, key_vecs, values, seg_row, live_cells, block_rows
    )
    attended = attended.reshape(length, model_width)
    middle = (
        cells_f
        + jnp.dot(attended, w_out, preferred_element_type=jnp.float32)
        + out_bias.astype(jnp.float32)
    )
    normed_two, inv_two = normalize(middle)
    hidden_in = (
        normed_two * norm2_gain.astype(jnp.float32) + norm2_bias.astype(jnp.float32)
    ).astype(jnp.bfloat16)
    pre_act = jnp.dot(hidden_in, w_up, preferred_element_type=jnp.float32) + up_bias.astype(
        jnp.float32
    )
    hidden = jax.nn.gelu(pre_act, approximate=False).astype(jnp.bfloat16)
    result = (
        middle
        + jnp.dot(hidden, w_down, preferred_element_type=jnp.float32)
        + down_bias.astype(jnp.float32)
    )
    kept = (
        normed_in,
        normed_one,
        inv_one,
        queries,
        key_vecs,
        values,
        attended,
        log_totals,
        normed_two,
        inv_two,
        hidden_in,
        pre_act,
        hidden,
    )
    return (result.astype(jnp.bfloat16), kept)


def backward_pass(gathered, kept, cotangent, seg_row, live_cells, block_rows):
    (
        w_qkv,
        query_bias,
        value_bias,
        w_out,
        out_bias,
        w_up,
        up_bias,
        w_down,
        down_bias,
        norm1_gain,
        norm1_bias,
        norm2_gain,
        norm2_bias,
    ) = gathered
    (
        normed_in,
        normed_one,
        inv_one,
        queries,
        key_vecs,
        values,
        attended,
        log_totals,
        normed_two,
        inv_two,
        hidden_in,
        pre_act,
        hidden,
    ) = kept
    length = attended.shape[0]
    upstream = cotangent.astype(jnp.float32)
    grad_down = jnp.einsum("tf,td->fd", hidden, cotangent, preferred_element_type=jnp.float32)
    grad_down_bias = jnp.sum(upstream, axis=0)
    hidden_grad = jnp.einsum("td,fd->tf", cotangent, w_down, preferred_element_type=jnp.float32)
    pre_grad = (hidden_grad * gelu_slope(pre_act)).astype(jnp.bfloat16)
    grad_up = jnp.einsum("td,tf->df", hidden_in, pre_grad, preferred_element_type=jnp.float32)
    grad_up_bias = jnp.sum(pre_grad.astype(jnp.float32), axis=0)
    mid_grad = jnp.einsum("tf,df->td", pre_grad, w_up, preferred_element_type=jnp.float32)
    grad_gain_two = jnp.sum(mid_grad * normed_two, axis=0)
    grad_shift_two = jnp.sum(mid_grad, axis=0)
    middle_grad = upstream + norm_back(
        mid_grad, normed_two, inv_two, norm2_gain.astype(jnp.float32)
    )
    branch_grad = middle_grad.astype(jnp.bfloat16)
    grad_out = jnp.einsum("td,te->de", attended, branch_grad, preferred_element_type=jnp.float32)
    grad_out_bias = jnp.sum(branch_grad.astype(jnp.float32), axis=0)
    attended_grad = jnp.einsum(
        "te,de->td", branch_grad, w_out, preferred_element_type=jnp.float32
    ).astype(jnp.bfloat16)
    query_grad, key_grad, value_grad = attention_backward(
        queries,
        key_vecs,
        values,
        attended_grad.reshape(queries.shape),
        log_totals,
        seg_row,
        live_cells,
        block_rows,
    )
    query_grad = query_grad.reshape(length, -1)
    value_grad = value_grad.reshape(length, -1)
    proj_grad = jnp.concatenate([query_grad, key_grad.reshape(length, -1), value_grad], axis=1)
    grad_qkv = jnp.einsum("td,te->de", normed_in, proj_grad, preferred_element_type=jnp.float32)
    grad_query_bias = jnp.sum(query_grad.astype(jnp.float32), axis=0)
    grad_value_bias = jnp.sum(value_grad.astype(jnp.float32), axis=0)
    in_grad = jnp.einsum("te,de->td", proj_grad, w_qkv, preferred_element_type=jnp.float32)
    grad_gain_one = jnp.sum(in_grad * normed_one, axis=0)
    grad_shift_one = jnp.sum(in_grad, axis=0)
    input_grad = (
        middle_grad + norm_back(in_grad, normed_one, inv_one, norm1_gain.astype(jnp.float32))
    ).astype(jnp.bfloat16)
    grads = (
        grad_qkv,
        grad_query_bias,
        grad_value_bias,
        grad_out,
        grad_out_bias,
        grad_up,
        grad_up_bias,
        grad_down,
        grad_down_bias,
        grad_gain_one,
        grad_shift_one,
        grad_gain_two,
        grad_shift_two,
    )
    return (input_grad, grads)


VECTORS = (1, 2, 4, 6, 8, 9, 10, 11, 12)
MATRICES = (0, 3, 5, 7)
EVERY = ("dp", "rep")


def gather_matrix(shard):
    part_rows = shard.shape[0] // lax.axis_size("rep")
    own = lax.dynamic_slice_in_dim(shard, lax.axis_index("rep") * part_rows, part_rows, 0)
    return lax.all_gather(own, EVERY, axis=0, tiled=True)


def gather_vectors(shards):
    packed = jnp.concatenate(shards)
    whole = lax.all_gather(packed, "dp", axis=0, tiled=False)
    vectors, begin = ([], 0)
    for shard in shards:
        vectors.append(whole[:, begin : begin + shard.shape[0]].reshape(-1))
        begin += shard.shape[0]
    return vectors


def reduce_matrix(grad):
    part = lax.psum_scatter(grad.astype(jnp.bfloat16), EVERY, scatter_dimension=0, tiled=True)
    return lax.all_gather(part, "rep", axis=0, tiled=True).astype(jnp.float32)


def reduce_vectors(grads):
    owners = lax.axis_size("dp")
    packed = jnp.concatenate([grad.reshape(owners, -1) for grad in grads], axis=1)
    total = lax.psum(packed, EVERY)
    own = lax.dynamic_index_in_dim(total, lax.axis_index("dp"), 0, keepdims=False)
    outs, begin = ([], 0)
    for grad in grads:
        size = grad.shape[0] // owners
        outs.append(own[begin : begin + size])
        begin += size
    return outs


def on_device(cell_input, cotangent, segment_ids, lengths, *shards):
    gathered = [None] * len(shards)
    for place, vector in zip(VECTORS, gather_vectors([shards[place] for place in VECTORS])):
        gathered[place] = vector
    for place in MATRICES:
        gathered[place] = gather_matrix(shards[place])
    length, model_width = cell_input.shape
    block_rows = min(length, 512)
    seg_row = segment_ids[0]
    live_cells = jnp.arange(length, dtype=jnp.int32) < lengths[0]
    pos_table = positions(length, model_width)
    block_out, kept = forward_pass(gathered, cell_input, pos_table, seg_row, live_cells, block_rows)
    input_grad, grads = backward_pass(gathered, kept, cotangent, seg_row, live_cells, block_rows)
    summed = [None] * len(grads)
    for place in (7, 5, 3, 0):
        summed[place] = reduce_matrix(grads[place])
    for place, vector in zip(VECTORS, reduce_vectors([grads[place] for place in VECTORS])):
        summed[place] = vector
    return (block_out, input_grad) + tuple(summed)


def solution(mesh):
    in_specs = (
        P(("dp", "rep"), None),
        P(("dp", "rep"), None),
        P(("dp", "rep"), None),
        P(("dp", "rep")),
        P("dp", None),
        P("dp"),
        P("dp"),
        P("dp", None),
        P("dp"),
        P("dp", None),
        P("dp"),
        P("dp", None),
        P("dp"),
        P("dp"),
        P("dp"),
        P("dp"),
        P("dp"),
    )
    out_specs = (
        P(("dp", "rep"), None),
        P(("dp", "rep"), None),
        P("dp", None),
        P("dp"),
        P("dp"),
        P("dp", None),
        P("dp"),
        P("dp", None),
        P("dp"),
        P("dp", None),
        P("dp"),
        P("dp"),
        P("dp"),
        P("dp"),
        P("dp"),
    )
    return jax.shard_map(
        on_device, mesh=mesh, in_specs=in_specs, out_specs=out_specs, check_vma=False
    )
```

profile of v0, /device:TPU:0, one launch (start us, length us, event | category | flops | bytes accessed | tf_op | source)
XLA Modules:
  0.0 915.2 jit_solution(13305810542900627797)
XLA Ops:
  7.2 1.7 constant_dynamic-slice_fusion.4
  9.0 1.5 constant_dynamic-slice_fusion.3
  11.4 1.7 constant_dynamic-slice_fusion.1
  21.3 32.7 %all-gather.1 = bf16[8,1,1536]{2,1,0:T(2,128)(2,1)S(1)} all-gather(bf16[1,1,1536]{2,1,0:T(2,128)(2,1)S(1)} %reshape.394), channel_id=2, replica_groups=mesh['dp'=8,'rep'=4] {'dp'}, dimensions={0}, use_global_device_ids=true | all-gather | bytes 27648 | tf_op jit(solution)/shard_map/all_gather | solution.py:303
  54.0 3.7 fusion.47
  58.0 2.6 copy.62
  60.6 3.7 reshape.368
  64.3 1.9 copy.63
  67.8 1.5 fusion.30
  69.3 14.1 %all-gather.9.cloned.1.call-done = bf16[1024,3072]{1,0:T(8,128)(2,1)} async-done(((bf16[32,3072]{1,0:T(8,128)(2,1)}), bf16[1024,3072]{1,0:T(8,128)(2,1)}) %all-gather.9.cloned.1.call-update) | async-done | bytes 6291472 | tf_op jit(solution)/shard_map/all_gather | solution.py:298
  83.4 5.8 fusion.65
  90.4 1.6 fusion.39
  92.5 1.9 copy.66
  94.4 2.7 copy.64
  97.1 7.4 fusion.63
  104.4 8.4 fusion
  112.9 8.9 fusion.41
  121.7 19.3 %all-gather.11.cloned.1.call-done = bf16[1024,1024]{1,0:T(8,128)(2,1)} async-done(((bf16[32,1024]{1,0:T(8,128)(2,1)}), bf16[1024,1024]{1,0:T(8,128)(2,1)}) %all-gather.11.cloned.1.call-update) | async-done | bytes 2097168 | tf_op jit(solution)/shard_map/all_gather | solution.py:298
  141.0 3.3 fusion.64
  144.7 75.7 %all-gather.13.cloned.1.call-done = bf16[1024,4096]{1,0:T(8,128)(2,1)} async-done(((bf16[32,4096]{1,0:T(8,128)(2,1)}), bf16[1024,4096]{1,0:T(8,128)(2,1)}) %all-gather.13.cloned.1.call-update) | async-done | bytes 8388624 | tf_op jit(solution)/shard_map/all_gather | solution.py:298
  220.4 27.0 %fusion.4 = (bf16[512,4096]{1,0:T(8,128)(2,1)}, f32[512,4096]{1,0:T(8,128)}) fusion(f32[4096]{0:T(1024)S(1)} %bitcast.148, bf16[1024,4096]{1,0:T(8,128)(2,1)} %all-gather.13.cloned.1.call-done, f32[512,1024]{1,0:T(8,128)S(1)} %get-tuple-element.106, f32[1024]{0:T(1024)S(1)} %get-tuple-element.94, f32[1024]{0:T(1024)S(1)} %get-tuple-element.95, ...), kind=kOutput, calls=%fused_computation.12 | convolution fusion | flops 4436000768 | bytes 23097344 | tf_op jit(solution)/shard_map/dot_general | solution.py:172
  247.4 51.4 %all-gather.15.cloned.1.call-done = bf16[4096,1024]{1,0:T(8,128)(2,1)} async-done(((bf16[128,1024]{1,0:T(8,128)(2,1)}), bf16[4096,1024]{1,0:T(8,128)(2,1)}) %all-gather.15.cloned.1.call-update) | async-done | bytes 8388624 | tf_op jit(solution)/shard_map/all_gather | solution.py:298
  298.8 11.3 %convert_reduce_fusion = (f32[4096]{0:T(1024)}, bf16[512,4096]{1,0:T(8,128)(2,1)S(1)}) fusion(f32[512,4096]{1,0:T(8,128)} %get-tuple-element.108, f32[4096]{0:T(1024)S(1)} %bitcast.149, bf16[4096,1024]{1,0:T(8,128)(2,1)} %all-gather.15.cloned.1.call-done, bf16[512,1024]{1,0:T(8,128)(2,1)S(1)} %copy-done.15), kind=kOutput, calls=%fused_computation.20 | convolution fusion | flops 4322226176 | bytes 22052864 | tf_op jit(solution)/shard_map/td,fd->tf/dot_general | solution.py:234
  310.1 2.0 copy-done.30
  312.1 7.3 convolution_convert_fusion.1
  319.5 9.1 convolution_convert_fusion
  329.3 9.4 %multiply_reduce_fusion.1 = (f32[1024]{0:T(1024)}, f32[512]{0:T(512)S(1)}, f32[512]{0:T(512)S(1)}, f32[1024]{0:T(1024)S(1)}, f32[512,1024]{1,0:T(8,128)S(1)}) fusion(f32[512,1024]{1,0:T(8,128)S(1)} %get-tuple-element.106, f32[512]{0:T(512)S(1)} %add_rsqrt_fusion, f32[512]{0:T(512)S(1)} %broadcast_multiply_fusion.4, f32[1024]{0:T(1024)S(1)} %get-tuple-element.95, ...), kind=kOutput, calls=%fused_computation.70 | convolution fusion | flops 4299682816 | bytes 16797696 | tf_op jit(solution)/shard_map/tf,df->td/dot_general | solution.py:238
  342.9 4.6 convolution_convert_fusion.3
  347.6 14.7 %multiply_reduce_fusion = (f32[16,512]{1,0:T(8,128)}, f32[16,512,512]{1,2,0:T(8,128)}) fusion(f32[16,512,512]{1,2,0:T(8,128)} %get-tuple-element.104, f32[16,512]{1,0:T(8,128)} %log_add_fusion, bf16[512,16,64]{0,2,1:T(8,128)(2,1)S(1)} %bitcast.134, bf16[512,16,64]{0,2,1:T(8,128)(2,1)} %bitcast.136), kind=kOutput, calls=%fused_computation.1 | convolution fusion | flops 549445632 | bytes 35717120 | tf_op jit(solution)/shard_map/while/body/eval_jaxpr/qhd,khd->hqk/dot_general | solution.py:92
  364.6 10.5 %multiply_convert_fusion = bf16[16,512,512]{1,2,0:T(8,128)(2,1)} fusion(f32[16,512,512]{1,2,0:T(8,128)} %get-tuple-element.111, f32[16,512,512]{1,2,0:T(8,128)S(1)} %bitcast.129, f32[16,512]{1,0:T(8,128)} %get-tuple-element.110, f32[16,512]{1,0:T(8,128)} %log_add_fusion), kind=kLoop, calls=%fused_computation | loop fusion | flops 16777216 | bytes 42008576 | tf_op jit(solution)/shard_map/while/body/eval_jaxpr/convert_element_type | solution.py:97
  375.2 6.6 multiply_convert_fusion.1
  381.8 1.5 convert_reduce_fusion.5
  383.3 8.9 convert_reduce_fusion.4
  393.1 8.4 convolution_convert_fusion.2
  402.8 8.5 fusion.36
  411.3 57.1 %reduce-scatter.9.cloned.1.call-done = bf16[32,4096]{1,0:T(8,128)(2,1)} async-done(((bf16[1024,4096]{1,0:T(8,128)(2,1)}), bf16[32,4096]{1,0:T(8,128)(2,1)}) %reduce-scatter.9.cloned.1.call-update) | async-done | bytes 262160 | tf_op jit(solution)/shard_map/reduce_scatter | solution.py:312
  468.5 40.1 %psum.7 = f32[8,1536]{1,0:T(8,128)S(1)} all-reduce(f32[8,1536]{1,0:T(8,128)S(1)} %constant_dynamic-update-slice_fusion), channel_id=1, replica_groups=mesh['dp'=8,'rep'=4] {'dp','rep'}, use_global_device_ids=true, to_apply=%region_21.22 | all-reduce | flops 12288 | bytes 98304 | tf_op jit(solution)/shard_map/psum | solution.py:319
  509.9 3.9 fusion.35
  513.9 102.6 %reduce-scatter.11.cloned.1.call-done = bf16[128,1024]{1,0:T(8,128)(2,1)} async-done(((bf16[4096,1024]{1,0:T(8,128)(2,1)}), bf16[128,1024]{1,0:T(8,128)(2,1)}) %reduce-scatter.11.cloned.1.call-update) | async-done | bytes 262160 | tf_op jit(solution)/shard_map/reduce_scatter | solution.py:312
  616.6 10.2 %add_convert_fusion = bf16[512,1024]{1,0:T(8,128)(2,1)} fusion(f32[512,1024]{1,0:T(8,128)S(1)} %copy-done.6, bf16[512,4096]{1,0:T(8,128)(2,1)} %get-tuple-element.107, bf16[4096,1024]{1,0:T(8,128)(2,1)} %all-gather.15.cloned.1.call-done, f32[1024]{0:T(1024)S(1)} %copy-done.28), kind=kOutput, calls=%fused_computation.77 | convolution fusion | flops 4296540160 | bytes 15732736 | tf_op jit(solution)/shard_map/dot_general | solution.py:178
  626.8 126.4 %reduce-scatter.7.cloned.1.call-done = bf16[32,1024]{1,0:T(8,128)(2,1)} async-done(((bf16[1024,1024]{1,0:T(8,128)(2,1)}), bf16[32,1024]{1,0:T(8,128)(2,1)}) %reduce-scatter.7.cloned.1.call-update) | async-done | bytes 65552 | tf_op jit(solution)/shard_map/reduce_scatter | solution.py:312
  753.2 6.0 all_gather.37
  760.0 109.7 %reduce-scatter.5.cloned.1.call-done = bf16[32,3072]{1,0:T(8,128)(2,1)} async-done(((bf16[1024,3072]{1,0:T(8,128)(2,1)}), bf16[32,3072]{1,0:T(8,128)(2,1)}) %reduce-scatter.5.cloned.1.call-update) | async-done | bytes 196624 | tf_op jit(solution)/shard_map/reduce_scatter | solution.py:312
  869.7 8.8 all_gather.36
  879.8 7.2 all-gather.17.cloned.1.call-done
  887.0 2.8 convert_element_type.255
  889.7 15.4 %all-gather.19.cloned.1.call-done = bf16[512,1024]{1,0:T(8,128)(2,1)} async-done(((bf16[128,1024]{1,0:T(8,128)(2,1)}), bf16[512,1024]{1,0:T(8,128)(2,1)}) %all-gather.19.cloned.1.call-update) | async-done | bytes 1048592 | tf_op jit(solution)/shard_map/all_gather | solution.py:313
  905.1 2.8 convert_element_type.257
  (142 shorter events, 25.3 us)
Async XLA Ops:
  7.2 3.4 copy-start
  7.2 76.2 %all-gather.9.cloned.1.call-start = ((), (), s32[]{:S(2)}) async-start(), calls=%async_computation.4 | async-start | bytes 6488064 | tf_op jit(solution)/shard_map/all_gather | solution.py:298
  9.0 132.1 %all-gather.11.cloned.1.call-start = ((), (), s32[]{:S(2)}) async-start(), calls=%async_computation.5 | async-start | bytes 2162688 | tf_op jit(solution)/shard_map/all_gather | solution.py:298
  10.5 209.9 %all-gather.13.cloned.1.call-start = ((), (), s32[]{:S(2)}) async-start(), calls=%async_computation.6 | async-start | bytes 8650752 | tf_op jit(solution)/shard_map/all_gather | solution.py:298
  11.3 287.5 %all-gather.15.cloned.1.call-start = ((), (), s32[]{:S(2)}) async-start(), calls=%async_computation.7 | async-start | bytes 8650752 | tf_op jit(solution)/shard_map/all_gather | solution.py:298
  13.1 455.3 %reduce-scatter.9.cloned.1.call-start = ((), (), s32[]{:S(2)}) async-start(), calls=%async_computation.10 | async-start | bytes 8650752 | tf_op jit(solution)/shard_map/reduce_scatter | solution.py:312
  58.0 8.3 copy-start.3
  60.6 6.9 copy-start.27
  66.5 22.7 %copy-start.22 = (f32[512]{0:T(512)}, f32[512]{0:T(512)S(1)}, u32[]{:S(2)}) copy-start(f32[512]{0:T(512)S(1)} %broadcast_multiply_fusion.5) | copy-start | bytes 6148
  66.9 22.3 %copy-start.24 = (f32[512]{0:T(512)}, f32[512]{0:T(512)S(1)}, u32[]{:S(2)}) copy-start(f32[512]{0:T(512)S(1)} %add_rsqrt_fusion.1) | copy-start | bytes 6148
  67.5 21.7 %copy-start.20 = (f32[1024]{0:T(1024)}, f32[1024]{0:T(1024)S(1)}, u32[]{:S(2)}) copy-start(f32[1024]{0:T(1024)S(1)} %get-tuple-element.100) | copy-start | bytes 12292
  92.5 11.9 %copy-start.9 = (bf16[512,1024]{0,1:T(8,128)(2,1)}, bf16[512,1024]{0,1:T(8,128)(2,1)S(1)}, u32[]{:S(2)}) copy-start(bf16[512,1024]{0,1:T(8,128)(2,1)S(1)} %copy.65) | copy-start | bytes 3145732
  94.4 10.1 %copy-start.7 = (bf16[512,1024]{0,1:T(8,128)(2,1)}, bf16[512,1024]{0,1:T(8,128)(2,1)S(1)}, u32[]{:S(2)}) copy-start(bf16[512,1024]{0,1:T(8,128)(2,1)S(1)} %copy.66) | copy-start | bytes 3145732
  104.4 8.4 copy-start.13
  144.3 194.4 %copy-start.5 = (f32[512,1024]{1,0:T(8,128)}, f32[512,1024]{1,0:T(8,128)S(1)}, u32[]{:S(2)}) copy-start(f32[512,1024]{1,0:T(8,128)S(1)} %get-tuple-element.106) | copy-start | bytes 6291460
  220.4 78.4 %copy-start.15 = (bf16[512,1024]{1,0:T(8,128)(2,1)S(1)}, bf16[512,1024]{1,0:T(8,128)(2,1)}, u32[]{:S(2)}) copy-start(bf16[512,1024]{1,0:T(8,128)(2,1)} %param.18) | copy-start | bytes 3145732
  310.1 2.0 copy-start.30
  319.5 297.0 %reduce-scatter.11.cloned.1.call-start = ((), (), s32[]{:S(2)}) async-start(), calls=%async_computation.12 | async-start | bytes 8650752 | tf_op jit(solution)/shard_map/reduce_scatter | solution.py:312
  328.6 424.6 %reduce-scatter.7.cloned.1.call-start = ((), (), s32[]{:S(2)}) async-start(), calls=%async_computation.9 | async-start | bytes 2162688 | tf_op jit(solution)/shard_map/reduce_scatter | solution.py:312
  338.7 2.3 copy-start.14
  339.7 1.3 copy-start.12
  339.7 3.2 copy-start.18
  342.9 19.5 %copy-start.10 = (bf16[512,1024]{0,1:T(8,128)(2,1)}, bf16[512,1024]{0,1:T(8,128)(2,1)S(1)}, u32[]{:S(2)}) copy-start(bf16[512,1024]{0,1:T(8,128)(2,1)S(1)} %copy.68) | copy-start | bytes 3145732
  347.5 522.1 %reduce-scatter.5.cloned.1.call-start = ((), (), s32[]{:S(2)}) async-start(), calls=%async_computation.8 | async-start | bytes 6488064 | tf_op jit(solution)/shard_map/reduce_scatter | solution.py:312
  347.6 14.8 %slice-start = ((s8[16777216]{0:T(1024)(128)(4,1)}), s8[4194304]{0:T(1024)(128)(4,1)S(1)}, s32[]{:S(2)}) async-start(s8[16777216]{0:T(1024)(128)(4,1)} %bitcast.128), calls=%async_computation.14 | async-start | bytes 8388608
  347.6 14.8 %slice-start.1 = ((s8[16777216]{0:T(1024)(128)(4,1)}), s8[4194304]{0:T(1024)(128)(4,1)S(1)}, s32[]{:S(2)}) async-start(s8[16777216]{0:T(1024)(128)(4,1)} %bitcast.128), calls=%async_computation.15 | async-start | bytes 8388608
  347.6 15.8 %slice-start.2 = ((s8[16777216]{0:T(1024)(128)(4,1)}), s8[4194304]{0:T(1024)(128)(4,1)S(1)}, s32[]{:S(2)}) async-start(s8[16777216]{0:T(1024)(128)(4,1)} %bitcast.128), calls=%async_computation.16 | async-start | bytes 8388608
  347.6 17.0 %slice-start.3 = ((s8[16777216]{0:T(1024)(128)(4,1)}), s8[4194304]{0:T(1024)(128)(4,1)S(1)}, s32[]{:S(2)}) async-start(s8[16777216]{0:T(1024)(128)(4,1)} %bitcast.128), calls=%async_computation.17 | async-start | bytes 8388608
  375.2 6.6 copy-start.2
  375.2 6.6 copy-start.8
  381.8 1.5 copy-start.11
  381.8 1.5 copy-start.19
  383.3 9.9 %copy-start.16 = (bf16[512,1024]{1,0:T(8,128)(2,1)S(1)}, bf16[512,1024]{1,0:T(8,128)(2,1)}, u32[]{:S(2)}) copy-start(bf16[512,1024]{1,0:T(8,128)(2,1)} %fusion.30) | copy-start | bytes 3145732
  392.2 1.0 copy-start.17
  401.5 0.7 copy-start.26
  401.5 1.2 copy-start.4
  401.5 1.2 copy-start.21
  401.5 1.2 copy-start.23
  401.5 1.2 copy-start.25
  401.6 485.4 %all-gather.17.cloned.1.call-start = ((), (), s32[]{:S(2)}) async-start(), calls=%async_computation.11 | async-start | bytes 1310720 | tf_op jit(solution)/shard_map/all_gather | solution.py:313
  402.8 65.7 %copy-start.29 = (f32[1024]{0:T(1024)S(1)}, f32[1024]{0:T(1024)}, u32[]{:S(2)}) copy-start(f32[1024]{0:T(1024)} %get-tuple-element.61) | copy-start | bytes 12292
  411.3 205.3 %copy-start.6 = (f32[512,1024]{1,0:T(8,128)S(1)}, f32[512,1024]{1,0:T(8,128)}, u32[]{:S(2)}) copy-start(f32[512,1024]{1,0:T(8,128)} %copy-done.5) | copy-start | bytes 6291460
  411.3 205.3 %copy-start.28 = (f32[1024]{0:T(1024)S(1)}, f32[1024]{0:T(1024)}, u32[]{:S(2)}) copy-start(f32[1024]{0:T(1024)} %get-tuple-element.93) | copy-start | bytes 12292
  468.4 436.6 %all-gather.19.cloned.1.call-start = ((), (), s32[]{:S(2)}) async-start(), calls=%async_computation.13 | async-start | bytes 1310720 | tf_op jit(solution)/shard_map/all_gather | solution.py:313
  616.5 291.3 %copy-start.1 = (bf16[128,4096]{1,0:T(8,128)(2,1)S(1)}, bf16[128,4096]{1,0:T(8,128)(2,1)}, u32[]{:S(2)}) copy-start(bf16[128,4096]{1,0:T(8,128)(2,1)} %param.26) | copy-start | bytes 3145732
Sparse Core Ops, SparseCore 0:
  11.4 71.9 all-gather.8
  86.3 54.7 all-gather.10
  144.5 75.8 all-gather.12
  223.1 75.6 all-gather.14
  319.6 148.7 reduce-scatter.8
  470.6 145.8 reduce-scatter.10
  618.8 134.3 reduce-scatter.6
  758.8 110.8 reduce-scatter.4
  871.3 15.6 all-gather.16
  888.4 16.6 all-gather.18
where the time goes:
time: 921 us; the launch traced here: 915 us
  waiting for transfers between devices  579 us (63%)
  matrix products  154 us (17%)
  blocking collectives  87.5 us (10%)
  other arithmetic  41.1 us (4%)
  local copies, waits for them, and re-layouts  36.9 us (4%)
  between operations  15.8 us (2%)
    reduce_scatter x4, waiting for transfers between devices, reduce_matrix(): lax.psum_scatter(grad.astype(jnp.bfloat16), EVERY, scatter_dimension=0, t...  396 us
    all_gather x4, waiting for transfers between devices, gather_matrix(): return lax.all_gather(own, EVERY, axis=0, tiled=True)  161 us
    psum x1, blocking collectives, reduce_vectors(): total = lax.psum(packed, EVERY)  40.1 us
    all_gather x1, blocking collectives, gather_vectors(): whole = lax.all_gather(packed, 'dp', axis=0, tiled=False)  32.7 us
    dot_general x1, matrix products, forward_pass(): jnp.dot(hidden_in, w_up, preferred_element_type=jnp.float32)  27 us
    all_gather x2, waiting for transfers between devices, reduce_matrix(): return lax.all_gather(part, 'rep', axis=0, tiled=True).astype(jnp.float32)  22.6 us
  transfers between devices with their start and end apart: 10, of which 10 were waited for; matrix products, arithmetic and copies ran while one was open for 22% of the time, Pallas kernels for 0%

commit v1 on v0

--- a/solution.py
+++ b/solution.py
@@ -316,7 +316,8 @@
 def reduce_vectors(grads):
     owners = lax.axis_size("dp")
     packed = jnp.concatenate([grad.reshape(owners, -1) for grad in grads], axis=1)
-    total = lax.psum(packed, EVERY)
+    last = lax.all_gather(packed, EVERY)
+    total = jnp.sum(last, axis=0)
     own = lax.dynamic_index_in_dim(total, lax.axis_index("dp"), 0, keepdims=False)
     outs, begin = ([], 0)
     for grad in grads:

time: 921 us -> 978 us (1.062)
  waiting for transfers between devices: 579 us -> 683 us
  blocking collectives: 87.5 us -> 47.4 us
    reduce_scatter x4, waiting for transfers between devices: 396 us -> 457 us  [reduce_matrix(): lax.psum_scatter(grad.astype(jnp.bfloat16), EVERY, scatter_dimension=0, t...]
    all_gather x0 -> x1, waiting for transfers between devices: none -> 42.1 us  [reduce_vectors(): last = lax.all_gather(packed, EVERY)]
    psum x1 -> x0, blocking collectives: 40.1 us -> none  [reduce_vectors(): total = lax.psum(packed, EVERY)]
  transfers between devices with their start and end apart: 10 -> 11, of which waited for: 10 -> 11; matrix products, arithmetic and copies ran while one was open for 22% -> 20% of each run, Pallas kernels for 0% -> 0%
where the time goes in v1:
time: 978 us; the launch traced here: 973 us
  waiting for transfers between devices  683 us (70%)
  matrix products  154 us (16%)
  blocking collectives  47.4 us (5%)
  other arithmetic  37.5 us (4%)
  local copies, waits for them, and re-layouts  34.9 us (4%)
  between operations  15.4 us (2%)
    reduce_scatter x4, waiting for transfers between devices, reduce_matrix(): lax.psum_scatter(grad.astype(jnp.bfloat16), EVERY, scatter_dimension=0, t...  457 us
    all_gather x4, waiting for transfers between devices, gather_matrix(): return lax.all_gather(own, EVERY, axis=0, tiled=True)  161 us
    all_gather x1, waiting for transfers between devices, reduce_vectors(): last = lax.all_gather(packed, EVERY)  42.1 us
    all_gather x1, blocking collectives, gather_vectors(): whole = lax.all_gather(packed, 'dp', axis=0, tiled=False)  32.7 us
    dot_general x1, matrix products, forward_pass(): jnp.dot(hidden_in, w_up, preferred_element_type=jnp.float32)  26.8 us
    all_gather x2, waiting for transfers between devices, reduce_matrix(): return lax.all_gather(part, 'rep', axis=0, tiled=True).astype(jnp.float32)  22.6 us
  transfers between devices with their start and end apart: 11, of which 11 were waited for; matrix products, arithmetic and copies ran while one was open for 20% of the time, Pallas kernels for 0%

profile of v1, /device:TPU:0, one launch (start us, length us, event | category | flops | bytes accessed | tf_op | source)
XLA Modules:
  0.0 972.7 jit_solution(1005191101161576677)
XLA Ops:
  7.2 1.7 constant_dynamic-slice_fusion.4
  11.4 1.7 constant_dynamic-slice_fusion.1
  21.3 32.7 %all-gather.2 = bf16[8,1,1536]{2,1,0:T(2,128)(2,1)S(1)} all-gather(bf16[1,1,1536]{2,1,0:T(2,128)(2,1)S(1)} %reshape.395), channel_id=2, replica_groups=mesh['dp'=8,'rep'=4] {'dp'}, dimensions={0}, use_global_device_ids=true | all-gather | bytes 27648 | tf_op jit(solution)/shard_map/all_gather | solution.py:303
  54.1 3.7 fusion.47
  58.0 2.6 copy.71
  60.6 3.7 reshape.368
  64.3 1.9 copy.72
  67.8 1.5 fusion.30
  69.3 14.1 %all-gather.11.cloned.1.call-done = bf16[1024,3072]{1,0:T(8,128)(2,1)} async-done(((bf16[32,3072]{1,0:T(8,128)(2,1)}), bf16[1024,3072]{1,0:T(8,128)(2,1)}) %all-gather.11.cloned.1.call-update) | async-done | bytes 6291472 | tf_op jit(solution)/shard_map/all_gather | solution.py:298
  83.4 5.8 fusion.65
  90.4 1.6 fusion.39
  92.5 1.9 copy.75
  94.4 2.7 copy.73
  97.1 7.4 fusion.63
  104.4 8.4 fusion
  112.9 8.7 fusion.41
  121.5 19.5 %all-gather.13.cloned.1.call-done = bf16[1024,1024]{1,0:T(8,128)(2,1)} async-done(((bf16[32,1024]{1,0:T(8,128)(2,1)}), bf16[1024,1024]{1,0:T(8,128)(2,1)}) %all-gather.13.cloned.1.call-update) | async-done | bytes 2097168 | tf_op jit(solution)/shard_map/all_gather | solution.py:298
  141.1 3.3 fusion.64
  144.7 75.7 %all-gather.15.cloned.1.call-done = bf16[1024,4096]{1,0:T(8,128)(2,1)} async-done(((bf16[32,4096]{1,0:T(8,128)(2,1)}), bf16[1024,4096]{1,0:T(8,128)(2,1)}) %all-gather.15.cloned.1.call-update) | async-done | bytes 8388624 | tf_op jit(solution)/shard_map/all_gather | solution.py:298
  220.4 26.8 %fusion.4 = (bf16[512,4096]{1,0:T(8,128)(2,1)}, f32[512,4096]{1,0:T(8,128)}) fusion(f32[4096]{0:T(1024)S(1)} %bitcast.148, bf16[1024,4096]{1,0:T(8,128)(2,1)} %all-gather.15.cloned.1.call-done, f32[512,1024]{1,0:T(8,128)S(1)} %get-tuple-element.106, f32[1024]{0:T(1024)S(1)} %get-tuple-element.94, f32[1024]{0:T(1024)S(1)} %get-tuple-element.95, ...), kind=kOutput, calls=%fused_computation.12 | convolution fusion | flops 4436000768 | bytes 23097344 | tf_op jit(solution)/shard_map/dot_general | solution.py:172
  247.3 51.6 %all-gather.17.cloned.1.call-done = bf16[4096,1024]{1,0:T(8,128)(2,1)} async-done(((bf16[128,1024]{1,0:T(8,128)(2,1)}), bf16[4096,1024]{1,0:T(8,128)(2,1)}) %all-gather.17.cloned.1.call-update) | async-done | bytes 8388624 | tf_op jit(solution)/shard_map/all_gather | solution.py:298
  298.8 12.1 %convert_reduce_fusion = (f32[4096]{0:T(1024)S(1)}, bf16[512,4096]{1,0:T(8,128)(2,1)S(1)}) fusion(f32[512,4096]{1,0:T(8,128)} %get-tuple-element.108, f32[4096]{0:T(1024)S(1)} %bitcast.149, bf16[4096,1024]{1,0:T(8,128)(2,1)} %all-gather.17.cloned.1.call-done, bf16[512,1024]{1,0:T(8,128)(2,1)} %param.18), kind=kOutput, calls=%fused_computation.20 | convolution fusion | flops 4322226176 | bytes 22052864 | tf_op jit(solution)/shard_map/td,fd->tf/dot_general | solution.py:234
  311.0 2.1 copy-done.35
  313.1 7.5 convolution_convert_fusion.1
  320.7 10.3 %convolution_convert_fusion = bf16[4096,1024]{1,0:T(8,128)(2,1)} fusion(bf16[512,4096]{1,0:T(8,128)(2,1)} %get-tuple-element.107, bf16[512,1024]{1,0:T(8,128)(2,1)} %param.18), kind=kOutput, calls=%fused_computation.38 | convolution fusion | flops 4299161600 | bytes 13631488 | tf_op jit(solution)/shard_map/tf,td->fd/dot_general | solution.py:232
  331.7 9.8 %multiply_reduce_fusion.1 = (f32[1024]{0:T(1024)}, f32[512]{0:T(512)S(1)}, f32[512]{0:T(512)S(1)}, f32[1024]{0:T(1024)}, f32[512,1024]{1,0:T(8,128)S(1)}) fusion(f32[512,1024]{1,0:T(8,128)S(1)} %get-tuple-element.106, f32[512]{0:T(512)S(1)} %add_rsqrt_fusion, f32[512]{0:T(512)S(1)} %broadcast_multiply_fusion.4, f32[1024]{0:T(1024)S(1)} %get-tuple-element.95, ...), kind=kOutput, calls=%fused_computation.70 | convolution fusion | flops 4299682816 | bytes 16797696 | tf_op jit(solution)/shard_map/tf,df->td/dot_general | solution.py:238
  345.6 9.9 %convert_reduce_fusion.4 = (f32[16,64]{1,0:T(8,128)S(1)}, bf16[16,64,512]{2,1,0:T(8,128)(2,1)}) fusion(bf16[512,16,64]{0,2,1:T(8,128)(2,1)S(1)} %bitcast.134, f32[16,512,512]{1,2,0:T(8,128)} %get-tuple-element.104, f32[16,512]{1,0:T(8,128)S(1)} %log_add_fusion), kind=kOutput, calls=%fused_computation.72 | convolution fusion | flops 546831360 | bytes 18911232 | tf_op jit(solution)/shard_map/while/body/eval_jaxpr/hqk,qhd->khd/dot_general | solution.py:86
  355.5 10.6 %multiply_reduce_fusion = (f32[16,512]{1,0:T(8,128)}, f32[16,512,512]{1,2,0:T(8,128)S(1)}) fusion(f32[16,512,512]{1,2,0:T(8,128)} %get-tuple-element.104, f32[16,512]{1,0:T(8,128)} %copy-done.22, bf16[512,16,64]{0,2,1:T(8,128)(2,1)} %bitcast.135, bf16[512,16,64]{0,2,1:T(8,128)(2,1)} %bitcast.136), kind=kOutput, calls=%fused_computation.1 | convolution fusion | flops 549445632 | bytes 35717120 | tf_op jit(solution)/shard_map/while/body/eval_jaxpr/qhd,khd->hqk/dot_general | solution.py:92
  366.1 8.3 multiply_convert_fusion
  374.5 2.9 convert_reduce_fusion.5
  378.1 6.2 multiply_convert_fusion.1
  384.4 8.9 fusion.36
  394.1 3.8 convolution_convert_fusion.3
  398.0 8.1 convolution_convert_fusion.2
  406.2 63.3 %reduce-scatter.9.cloned.1.call-done = bf16[32,4096]{1,0:T(8,128)(2,1)} async-done(((bf16[1024,4096]{1,0:T(8,128)(2,1)}), bf16[32,4096]{1,0:T(8,128)(2,1)}) %reduce-scatter.9.cloned.1.call-update) | async-done | bytes 262160 | tf_op jit(solution)/shard_map/reduce_scatter | solution.py:312
  469.8 147.7 %reduce-scatter.11.cloned.1.call-done = bf16[128,1024]{1,0:T(8,128)(2,1)} async-done(((bf16[4096,1024]{1,0:T(8,128)(2,1)}), bf16[128,1024]{1,0:T(8,128)(2,1)}) %reduce-scatter.11.cloned.1.call-update) | async-done | bytes 262160 | tf_op jit(solution)/shard_map/reduce_scatter | solution.py:312
  617.6 10.3 %add_convert_fusion = bf16[512,1024]{1,0:T(8,128)(2,1)} fusion(f32[512,1024]{1,0:T(8,128)S(1)} %copy-done.6, bf16[512,4096]{1,0:T(8,128)(2,1)} %get-tuple-element.107, bf16[4096,1024]{1,0:T(8,128)(2,1)} %all-gather.17.cloned.1.call-done, f32[1024]{0:T(1024)S(1)} %copy-done.32), kind=kOutput, calls=%fused_computation.77 | convolution fusion | flops 4296540160 | bytes 15732736 | tf_op jit(solution)/shard_map/dot_general | solution.py:178
  627.9 1.7 fusion.35
  629.7 42.1 %all-gather.23.cloned.1.call-done = f32[256,1536]{1,0:T(8,128)} async-done(((f32[8,1536]{1,0:T(8,128)}), f32[256,1536]{1,0:T(8,128)}) %all-gather.23.cloned.1.call-update) | async-done | bytes 1572880 | tf_op jit(solution)/shard_map/all_gather | solution.py:319
  671.7 1.5 bitcast_reduce_fusion
  674.5 136.7 %reduce-scatter.7.cloned.1.call-done = bf16[32,1024]{1,0:T(8,128)(2,1)} async-done(((bf16[1024,1024]{1,0:T(8,128)(2,1)}), bf16[32,1024]{1,0:T(8,128)(2,1)}) %reduce-scatter.7.cloned.1.call-update) | async-done | bytes 65552 | tf_op jit(solution)/shard_map/reduce_scatter | solution.py:312
  811.2 6.0 all_gather.45
  818.0 109.7 %reduce-scatter.5.cloned.1.call-done = bf16[32,3072]{1,0:T(8,128)(2,1)} async-done(((bf16[1024,3072]{1,0:T(8,128)(2,1)}), bf16[32,3072]{1,0:T(8,128)(2,1)}) %reduce-scatter.5.cloned.1.call-update) | async-done | bytes 196624 | tf_op jit(solution)/shard_map/reduce_scatter | solution.py:312
  927.7 8.8 all_gather.42
  937.8 7.0 all-gather.19.cloned.1.call-done
  944.8 2.8 convert_element_type.255
  947.6 15.5 %all-gather.21.cloned.1.call-done = bf16[512,1024]{1,0:T(8,128)(2,1)} async-done(((bf16[128,1024]{1,0:T(8,128)(2,1)}), bf16[512,1024]{1,0:T(8,128)(2,1)}) %all-gather.21.cloned.1.call-update) | async-done | bytes 1048592 | tf_op jit(solution)/shard_map/all_gather | solution.py:313
  963.1 2.8 convert_element_type.257
  (146 shorter events, 24.1 us)
Async XLA Ops:
  7.2 3.4 copy-start
  7.2 76.2 %all-gather.11.cloned.1.call-start = ((), (), s32[]{:S(2)}) async-start(), calls=%async_computation.4 | async-start | bytes 6488064 | tf_op jit(solution)/shard_map/all_gather | solution.py:298
  9.0 132.1 %all-gather.13.cloned.1.call-start = ((), (), s32[]{:S(2)}) async-start(), calls=%async_computation.5 | async-start | bytes 2162688 | tf_op jit(solution)/shard_map/all_gather | solution.py:298
  10.5 209.9 %all-gather.15.cloned.1.call-start = ((), (), s32[]{:S(2)}) async-start(), calls=%async_computation.6 | async-start | bytes 8650752 | tf_op jit(solution)/shard_map/all_gather | solution.py:298
  11.3 287.5 %all-gather.17.cloned.1.call-start = ((), (), s32[]{:S(2)}) async-start(), calls=%async_computation.7 | async-start | bytes 8650752 | tf_op jit(solution)/shard_map/all_gather | solution.py:298
  13.1 456.4 %reduce-scatter.9.cloned.1.call-start = ((), (), s32[]{:S(2)}) async-start(), calls=%async_computation.10 | async-start | bytes 8650752 | tf_op jit(solution)/shard_map/reduce_scatter | solution.py:312
  58.0 8.2 copy-start.3
  60.6 6.9 copy-start.31
  66.5 22.7 %copy-start.27 = (f32[512]{0:T(512)}, f32[512]{0:T(512)S(1)}, u32[]{:S(2)}) copy-start(f32[512]{0:T(512)S(1)} %broadcast_multiply_fusion.5) | copy-start | bytes 6148
  66.9 22.3 %copy-start.29 = (f32[512]{0:T(512)}, f32[512]{0:T(512)S(1)}, u32[]{:S(2)}) copy-start(f32[512]{0:T(512)S(1)} %add_rsqrt_fusion.1) | copy-start | bytes 6148
  67.5 21.7 %copy-start.25 = (f32[1024]{0:T(1024)}, f32[1024]{0:T(1024)S(1)}, u32[]{:S(2)}) copy-start(f32[1024]{0:T(1024)S(1)} %get-tuple-element.100) | copy-start | bytes 12292
  92.5 12.0 %copy-start.9 = (bf16[512,1024]{0,1:T(8,128)(2,1)}, bf16[512,1024]{0,1:T(8,128)(2,1)S(1)}, u32[]{:S(2)}) copy-start(bf16[512,1024]{0,1:T(8,128)(2,1)S(1)} %copy.74) | copy-start | bytes 3145732
  94.4 10.1 %copy-start.7 = (bf16[512,1024]{0,1:T(8,128)(2,1)}, bf16[512,1024]{0,1:T(8,128)(2,1)S(1)}, u32[]{:S(2)}) copy-start(bf16[512,1024]{0,1:T(8,128)(2,1)S(1)} %copy.75) | copy-start | bytes 3145732
  104.4 8.4 copy-start.15
  144.3 197.1 %copy-start.5 = (f32[512,1024]{1,0:T(8,128)}, f32[512,1024]{1,0:T(8,128)S(1)}, u32[]{:S(2)}) copy-start(f32[512,1024]{1,0:T(8,128)S(1)} %get-tuple-element.106) | copy-start | bytes 6291460
  311.0 2.1 copy-start.35
  320.6 296.9 %reduce-scatter.11.cloned.1.call-start = ((), (), s32[]{:S(2)}) async-start(), calls=%async_computation.12 | async-start | bytes 8650752 | tf_op jit(solution)/shard_map/reduce_scatter | solution.py:312
  331.0 340.8 %all-gather.23.cloned.1.call-start = ((), (), s32[]{:S(2)}) async-start(), calls=%async_computation.14 | async-start | bytes 1622016 | tf_op jit(solution)/shard_map/all_gather | solution.py:319
  331.0 14.5 %copy-start.22 = (f32[16,512]{1,0:T(8,128)}, f32[16,512]{1,0:T(8,128)S(1)}, u32[]{:S(2)}) copy-start(f32[16,512]{1,0:T(8,128)S(1)} %log_add_fusion) | copy-start | bytes 98308
  331.7 9.8 %copy-start.20 = (bf16[512,1024]{1,0:T(8,128)(2,1)S(1)}, bf16[512,1024]{1,0:T(8,128)(2,1)}, u32[]{:S(2)}) copy-start(bf16[512,1024]{1,0:T(8,128)(2,1)} %param.18) | copy-start | bytes 3145732
  341.4 2.3 copy-start.18
  342.3 1.3 copy-start.12
  345.5 9.9 %copy-start.11 = (bf16[512,1024]{0,1:T(8,128)(2,1)}, bf16[512,1024]{0,1:T(8,128)(2,1)S(1)}, u32[]{:S(2)}) copy-start(bf16[512,1024]{0,1:T(8,128)(2,1)S(1)} %copy.77) | copy-start | bytes 3145732
  366.1 8.3 copy-start.8
  374.4 3.6 copy-start.2
  374.4 3.6 copy-start.23
  374.5 3.7 copy-start.10
  378.0 6.4 copy-start.26
  378.0 6.4 copy-start.28
  378.0 6.4 copy-start.30
  378.1 6.3 copy-start.16
  384.3 9.0 copy-start.21
  384.4 9.0 copy-start.34
  384.4 9.0 copy-start.33
  384.4 9.7 copy-start.13
  393.4 0.6 copy-start.24
  393.4 4.6 copy-start.17
  394.1 417.1 %reduce-scatter.7.cloned.1.call-start = ((), (), s32[]{:S(2)}) async-start(), calls=%async_computation.9 | async-start | bytes 2162688 | tf_op jit(solution)/shard_map/reduce_scatter | solution.py:312
  398.0 529.7 %reduce-scatter.5.cloned.1.call-start = ((), (), s32[]{:S(2)}) async-start(), calls=%async_computation.8 | async-start | bytes 6488064 | tf_op jit(solution)/shard_map/reduce_scatter | solution.py:312
  406.1 211.5 %copy-start.6 = (f32[512,1024]{1,0:T(8,128)S(1)}, f32[512,1024]{1,0:T(8,128)}, u32[]{:S(2)}) copy-start(f32[512,1024]{1,0:T(8,128)} %copy-done.5) | copy-start | bytes 6291460
  406.1 211.5 %copy-start.32 = (f32[1024]{0:T(1024)S(1)}, f32[1024]{0:T(1024)}, u32[]{:S(2)}) copy-start(f32[1024]{0:T(1024)} %get-tuple-element.93) | copy-start | bytes 12292
  406.1 538.7 %all-gather.19.cloned.1.call-start = ((), (), s32[]{:S(2)}) async-start(), calls=%async_computation.11 | async-start | bytes 1310720 | tf_op jit(solution)/shard_map/all_gather | solution.py:313
  469.5 493.6 %all-gather.21.cloned.1.call-start = ((), (), s32[]{:S(2)}) async-start(), calls=%async_computation.13 | async-start | bytes 1310720 | tf_op jit(solution)/shard_map/all_gather | solution.py:313
  617.6 10.3 %copy-start.4 = (bf16[512,1024]{1,0:T(8,128)(2,1)S(1)}, bf16[512,1024]{1,0:T(8,128)(2,1)}, u32[]{:S(2)}) copy-start(bf16[512,1024]{1,0:T(8,128)(2,1)} %param.17) | copy-start | bytes 3145732
  617.6 10.3 %copy-start.14 = (f32[512,1024]{1,0:T(8,128)S(1)}, f32[512,1024]{1,0:T(8,128)}, u32[]{:S(2)}) copy-start(f32[512,1024]{1,0:T(8,128)} %copy-done.12) | copy-start | bytes 6291460
  617.6 10.3 %copy-start.19 = (f32[512,1024]{1,0:T(8,128)S(1)}, f32[512,1024]{1,0:T(8,128)}, u32[]{:S(2)}) copy-start(f32[512,1024]{1,0:T(8,128)} %get-tuple-element.112) | copy-start | bytes 6291460
  627.9 338.0 %copy-start.1 = (bf16[128,4096]{1,0:T(8,128)(2,1)S(1)}, bf16[128,4096]{1,0:T(8,128)(2,1)}, u32[]{:S(2)}) copy-start(bf16[128,4096]{1,0:T(8,128)(2,1)} %param.26) | copy-start | bytes 3145732
Sparse Core Ops, SparseCore 0:
  11.4 71.9 all-gather.10
  86.3 54.7 all-gather.12
  144.5 75.8 all-gather.14
  223.1 75.6 all-gather.16
  320.8 148.6 reduce-scatter.8
  471.6 145.8 reduce-scatter.10
  621.0 50.6 all-gather.22
  674.0 137.1 reduce-scatter.6
  816.8 110.8 reduce-scatter.4
  929.1 15.6 all-gather.18
  946.4 16.6 all-gather.20
